TPU v7x, 256 devices: a whole 4x4x8 slice. The times are simulated.
256 devices in a mesh: layer: 8 (over y_lo, x), feat: 32 (over z, y_hi, core).
Axes of the slice: x: 4, y: 4 (y_hi: 2, y_lo: 2; y = y_hi * 2 + y_lo), z: 8, core: 2. Of those that a mesh axis runs over, the one named last changes fastest.
Arguments:
- inputs: bfloat16 [8, 128, 2304], P('layer'), may hold values from -6 to 6
- targets: bfloat16 [8, 128, 2304], P('layer', None, 'feat'), may hold values from -6 to 6
- w_enc: bfloat16 [8, 2304, 2048], P('layer', None, 'feat'), may hold values from -0.125 to 0.125
- b_enc: float32 [8, 2048], P('layer', 'feat'), may hold values from -3 to 3
- w_dec: bfloat16 [8, 8, 2048, 2304], P('layer', None, 'feat'), may hold values from -0.046875 to 0.046875
Outputs:
- grad_enc: bfloat16 [8, 2304, 2048], P('layer', None, 'feat')
- grad_dec: bfloat16 [8, 8, 2048, 2304], P('layer', None, 'feat')
- grad_benc: float32 [8, 2048], P('layer', 'feat')
All inputs are finite; a program needn't handle non-finite values.
Results may differ from a plain program's by a relative error of at most 0.0085.
Values may be sent and summed in bfloat16 or wider, within the bound.
A program may use at most 64 MiB of HBM per device.

v0:
```python
import jax
import jax.numpy as jnp
from jax import lax
from jax.sharding import PartitionSpec as P


def shards(inputs, targets, w_enc, b_enc, w_dec):
    layer_count = w_dec.shape[1]
    feat_count = lax.axis_size("feat")
    tok_count = inputs.shape[1]
    model_width = inputs.shape[2]
    col_count = model_width // feat_count
    slab_width = w_dec.shape[2]
    grad_scale = tok_count ** (-0.5)
    own_layer = lax.axis_index("layer")
    pre_act = jnp.dot(inputs[0], w_enc[0], preferred_element_type=jnp.float32) + b_enc[0]
    active = jax.nn.relu(pre_act).astype(jnp.bfloat16)
    later_mask = jnp.arange(layer_count) >= own_layer
    later_float = later_mask.astype(jnp.float32)
    later_half = later_mask.astype(jnp.bfloat16)
    weights = w_dec[0]
    blocks = weights.reshape(layer_count, slab_width, feat_count, col_count)
    partials = jnp.einsum("tf,mfnc->mntc", active, blocks, preferred_element_type=jnp.float32)
    partials = partials * later_float[:, None, None, None]
    partials = partials.reshape(layer_count * feat_count, tok_count, col_count)
    rebuilt = lax.psum_scatter(partials, ("layer", "feat"), scatter_dimension=0, tiled=True)[0]
    errors = (rebuilt - targets[0].astype(jnp.float32)).astype(jnp.bfloat16)
    err_block = errors[None, None]
    everything = lax.all_gather(err_block, ("layer", "feat"), axis=0, tiled=True)
    everything = everything.reshape(layer_count, feat_count, tok_count, col_count)
    masked = everything * later_half[:, None, None, None]
    act_grad = grad_scale * jnp.einsum(
        "mntc,mfnc->tf", masked, blocks, preferred_element_type=jnp.float32
    )
    dec_grad = (
        jnp.einsum("tf,mntc->mfnc", active, masked, preferred_element_type=jnp.float32) * grad_scale
    )
    grad_dec = dec_grad.astype(jnp.bfloat16).reshape(layer_count, slab_width, model_width)
    pre_grad = jnp.where(pre_act > 0, act_grad, 0.0).astype(jnp.bfloat16)
    grad_enc = jnp.einsum(
        "td,tf->df", inputs[0], pre_grad, preferred_element_type=jnp.float32
    ).astype(jnp.bfloat16)
    grad_benc = jnp.sum(pre_grad.astype(jnp.float32), axis=0)
    return (grad_enc[None], grad_dec[None], grad_benc[None])


def solution(mesh):
    in_specs = (
        P("layer", None, None),
        P("layer", None, "feat"),
        P("layer", None, "feat"),
        P("layer", "feat"),
        P("layer", None, "feat", None),
    )
    out_specs = (P("layer", None, "feat"), P("layer", None, "feat", None), P("layer", "feat"))
    return jax.shard_map(shards, mesh=mesh, in_specs=in_specs, out_specs=out_specs, check_vma=False)
```

profile of v0, /device:TPU:32, one launch (start us, length us, event | category | flops | bytes accessed | tf_op | source)
XLA Modules:
  0.0 1771.0 jit_solution(4785494572840686136)
XLA Ops:
  7.2 0.0 copy-start
  7.2 0.0 copy-start.4
  7.2 0.0 copy-start.2
  7.2 0.0 reduce-scatter.5.cloned.1.call-start
  7.3 11.4 reshape_squeeze.3
  18.6 0.0 copy-done
  18.6 0.0 copy-done.4
  18.6 0.0 copy-done.2
  18.6 0.3 convolution_add_fusion
  19.0 8.7 broadcast_multiply_fusion
  27.6 0.0 copy-start.3
  27.7 0.0 reduce-scatter.5.cloned.1.call-update
  27.7 0.2 all-gather.3.cloned.1.call-start
  27.9 1287.9 %reduce-scatter.5.cloned.1.call-done = f32[1,128,72]{1,2,0:T(8,128)} async-done(((f32[256,128,72]{1,2,0:T(8,128)}), f32[1,128,72]{1,2,0:T(8,128)}) %reduce-scatter.5.cloned.1.call-update) | async-done | bytes 36880
  1315.8 0.0 copy-done.3
  1315.8 1.4 subtract_convert_fusion
  1317.2 0.0 all-gather.3.cloned.1.call-update
  1317.3 421.7 %all-gather.3.cloned.1.call-done = bf16[256,128,72]{1,2,0:T(8,128)(2,1)} async-done(((bf16[1,128,72]{1,2,0:T(8,128)(2,1)}), bf16[256,128,72]{1,2,0:T(8,128)(2,1)}) %all-gather.3.cloned.1.call-update) | async-done | bytes 4718608 | tf_op jit(solution)/shard_map/all_gather | solution.py:29
  1738.9 0.0 copy-start.1
  1738.9 7.0 convert_reduce_fusion
  1746.0 0.0 copy-done.1
  1746.0 4.3 fusion
  1750.3 4.8 copy.15
  1755.1 8.1 broadcast_in_dim_reshape.3
  1763.2 0.9 fusion.10
  (2 shorter events, 0.0 us)
Async XLA Ops:
  7.2 11.5 copy-start
  7.2 11.4 copy-start.4
  7.2 11.4 copy-start.2
  7.2 1308.6 %reduce-scatter.5.cloned.1.call-start = ((), (), s32[]{:S(2)}) async-start(), calls=%async_computation.2 | async-start | bytes 9474048
  27.6 1288.2 %copy-start.3 = (bf16[1,128,72]{1,2,0:T(8,128)(2,1)S(1)}, bf16[1,128,72]{1,2,0:T(8,128)(2,1)}, u32[]{:S(2)}) copy-start(bf16[1,128,72]{1,2,0:T(8,128)(2,1)} %param.6) | copy-start | bytes 55300
  27.7 1711.3 %all-gather.3.cloned.1.call-start = ((), (), s32[]{:S(2)}) async-start(), calls=%async_computation.1 | async-start | bytes 4737024 | tf_op jit(solution)/shard_map/all_gather | solution.py:29
  1738.9 7.0 copy-start.1
Sparse Core Ops, SparseCore 0:
  27.8 1287.9 reduce-scatter.4
  1318.3 420.5 all-gather.2
where the time goes:
time: 1770 us
  waiting for transfers between devices  1710 us (97%)
  local copies, waits for them, and re-layouts  24.3 us (1%)
  matrix products  21.3 us (1%)
    unnamed x3, waiting for transfers between devices  1290 us
    all_gather x1, waiting for transfers between devices, shards(): lax.all_gather(err_block, ('layer', 'feat'), axis=0, tiled=True)  422 us
  transfers between devices with their start and end apart: 2, of which 2 were waited for; matrix products, arithmetic and copies ran while one was open for 0% of the time, Pallas kernels for 0%

commit v1 on v0

--- a/solution.py
+++ b/solution.py
@@ -2,6 +2,7 @@
 import jax.numpy as jnp
 from jax import lax
 from jax.sharding import PartitionSpec as P
+from jax.lax import all_to_all, axis_size
 
 
 def shards(inputs, targets, w_enc, b_enc, w_dec):
@@ -26,7 +27,15 @@
     rebuilt = lax.psum_scatter(partials, ("layer", "feat"), scatter_dimension=0, tiled=True)[0]
     errors = (rebuilt - targets[0].astype(jnp.float32)).astype(jnp.bfloat16)
     err_block = errors[None, None]
-    everything = lax.all_gather(err_block, ("layer", "feat"), axis=0, tiled=True)
+    everything = jnp.concatenate(
+        all_to_all(
+            jnp.stack(axis_size(("layer", "feat")) * [err_block]),
+            split_axis=0,
+            concat_axis=0,
+            axis_name=("layer", "feat"),
+        ),
+        0,
+    )
     everything = everything.reshape(layer_count, feat_count, tok_count, col_count)
     masked = everything * later_half[:, None, None, None]
     act_grad = grad_scale * jnp.einsum(

time: 1770 us -> 1490 us (0.84)
  waiting for transfers between devices: 1710 us -> 1400 us
  starting transfers between devices: 0.26 us -> 19.3 us
    all_gather x1 -> x0, waiting for transfers between devices: 422 us -> none  [shards(): lax.all_gather(err_block, ('layer', 'feat'), axis=0, tiled=True)]
    all_to_all x0 -> x1, waiting for transfers between devices: none -> 107 us  [shards(): all_to_all(jnp.stack(axis_size(('layer', 'feat')) * [err_block]), split_a...]
    all_to_all x0 -> x1, starting transfers between devices: none -> 19.2 us  [shards(): all_to_all(jnp.stack(axis_size(('layer', 'feat')) * [err_block]), split_a...]
    unnamed x3 -> x2, waiting for transfers between devices: 1290 us -> 1290 us
where the time goes in v1:
time: 1490 us; the launch traced here: 1480 us
  waiting for transfers between devices  1400 us (94%)
  local copies, waits for them, and re-layouts  27 us (2%)
  matrix products  23.5 us (2%)
  starting transfers between devices  19.3 us (1%)
    unnamed x2, waiting for transfers between devices  1290 us
    all_to_all x1, waiting for transfers between devices, shards(): all_to_all(jnp.stack(axis_size(('layer', 'feat')) * [err_block]), split_a...  107 us
  transfers between devices with their start and end apart: 2, of which 2 were waited for; matrix products, arithmetic and copies ran while one was open for 0% of the time, Pallas kernels for 0%

profile of v1, /device:TPU:32, one launch (start us, length us, event | category | flops | bytes accessed | tf_op | source)
XLA Modules:
  0.0 1483.4 jit_solution(3741980360788733408)
XLA Ops:
  7.2 0.0 copy-start
  7.2 0.0 copy-start.3
  7.2 0.0 copy-start.1
  7.2 0.0 reduce-scatter.5.cloned.1.call-start
  7.3 11.3 reshape_squeeze.3
  18.6 0.0 copy-done
  18.6 0.0 copy-done.3
  18.6 0.0 copy-done.1
  18.6 0.3 convolution_add_fusion
  19.0 8.7 broadcast_multiply_fusion
  27.6 0.0 copy-start.2
  27.6 0.0 reduce-scatter.5.cloned.1.call-update
  27.7 1291.6 %reduce-scatter.5.cloned.1.call-done = f32[1,128,72]{1,2,0:T(8,128)} async-done(((f32[256,128,72]{1,2,0:T(8,128)}), f32[1,128,72]{1,2,0:T(8,128)}) %reduce-scatter.5.cloned.1.call-update) | async-done | bytes 36880
  1319.3 0.0 copy-done.2
  1319.3 0.8 fusion.38
  1320.1 2.8 stack.3
  1322.8 19.2 %all-to-all-start = ((bf16[256,1,1,128,72]{3,4,2,1,0:T(8,128)(2,1)}), bf16[256,1,1,128,72]{3,4,2,1,0:T(8,128)(2,1)}, u32[]{:S(2)}, u32[]{:S(2)}) async-start(bf16[256,1,1,128,72]{3,4,2,1,0:T(8,128)(2,1)} %stack.3), calls=%async_computation | async-start | bytes 9437184 | tf_op jit(solution)/shard_map/all_to_all | solution.py:31
  1342.1 107.0 %all-to-all-done = bf16[256,1,1,128,72]{3,4,2,1,0:T(8,128)(2,1)} async-done(((bf16[256,1,1,128,72]{3,4,2,1,0:T(8,128)(2,1)}), bf16[256,1,1,128,72]{3,4,2,1,0:T(8,128)(2,1)}, u32[]{:S(2)}, u32[]{:S(2)}) %all-to-all-start) | async-done | bytes 4718624 | tf_op jit(solution)/shard_map/all_to_all | solution.py:31
  1449.1 6.9 convert_reduce_fusion
  1456.0 6.7 fusion
  1462.7 4.8 copy.15
  1467.5 8.1 broadcast_in_dim_reshape.3
  1475.6 0.9 fusion.10
  (2 shorter events, 0.0 us)
Async XLA Ops:
  7.2 11.4 copy-start
  7.2 11.4 copy-start.3
  7.2 11.4 copy-start.1
  7.2 1312.1 %reduce-scatter.5.cloned.1.call-start = ((), (), s32[]{:S(2)}) async-start(), calls=%async_computation.2 | async-start | bytes 9474048
  27.6 1291.6 %copy-start.2 = (bf16[1,128,72]{1,2,0:T(8,128)(2,1)S(1)}, bf16[1,128,72]{1,2,0:T(8,128)(2,1)}, u32[]{:S(2)}) copy-start(bf16[1,128,72]{1,2,0:T(8,128)(2,1)} %param.6) | copy-start | bytes 55300
  1322.8 126.3 %all-to-all-start = ((bf16[256,1,1,128,72]{3,4,2,1,0:T(8,128)(2,1)}), bf16[256,1,1,128,72]{3,4,2,1,0:T(8,128)(2,1)}, u32[]{:S(2)}, u32[]{:S(2)}) async-start(bf16[256,1,1,128,72]{3,4,2,1,0:T(8,128)(2,1)} %stack.3), calls=%async_computation | async-start | bytes 9437184 | tf_op jit(solution)/shard_map/all_to_all | solution.py:31
Sparse Core Ops, SparseCore 0:
  27.8 1291.4 reduce-scatter.4
